TPU v7x, 128 devices: a whole 4x4x4 slice. The times are simulated.
128 devices in a mesh: req: 32 (over z, x, core), tp: 4 (over y).
Axes of the slice: x: 4, y: 4, z: 4, core: 2. Of those that a mesh axis runs over, the one named last changes fastest.
Arguments:
- tokens: bfloat16 [12288, 5120], P('req'), may hold values from -40 to 40
- w_query: bfloat16 [5120, 2560], P(None, 'tp'), may hold values from -0.125 to 0.125
- query_bias: float32 [2560], P('tp'), may hold values from -24 to 24
- w_keyval: bfloat16 [5120, 1024], P(None, 'tp'), may hold values from -0.21875 to 0.21875
- keyval_bias: float32 [1024], P('tp'), may hold values from -2.5 to 2.5
- w_out: bfloat16 [2560, 5120], P('tp'), may hold values from -0.25 to 0.25
- attn_gain: float32 [5120], replicated, may hold values from 0.25 to 1.75
- final_norm_gain: float32 [5120], replicated, may hold values from 0.25 to 1.75
- head_weight: bfloat16 [5120, 76032], P(None, ('req', 'tp')), may hold values from -0.25 to 0.25
- kv_pool: bfloat16 [851968, 4, 256], P('req', 'tp'), may hold values from -17 to 17
- cache_len: int32 [512], replicated, may hold values from 256 to 3072, as said below
Outputs:
- states: bfloat16 [12288, 5120], P('req', 'tp')
- new_kv: bfloat16 [12288, 4, 256], P('req', 'tp')
- row_norms: float32 [512], P('req')
- logit_max: float32 [512], replicated
- logits: float32 [512, 76032], P(None, ('req', 'tp'))
Inputs may be any that keep to these rules, and one draw needn't show every extreme that they name: `cache_len`: every cache holds 256 or 3072 rows. Exactly 64 requests hold 3072; requests i * 16 to i * 16 + 15 hold at most 8 of them for every i, and exactly 8 for some i, so their caches fill at most 26624 rows, and exactly 26624 for some i.
All inputs are finite; a program needn't handle non-finite values.
Results may differ from a plain program's by a relative error of at most 0.014.
Values may be sent and summed in bfloat16 or wider, within the bound.
A program may use at most 192 MiB of HBM per device.

v0:
```python
import math
import jax
import jax.numpy as jnp
from jax import lax
from jax.sharding import PartitionSpec as P

HD = 128
GROUP = 5
NEW = 24
LONG = 3072
THETA = 1000000.0
EPS = 1e-06
NEG = -1e30


def rope_rotate(vectors, positions):
    head_width = vectors.shape[-1]
    halfway = head_width // 2
    frequency = THETA ** (-(jnp.arange(halfway, dtype=jnp.float32) * (2.0 / head_width)))
    angles = positions[..., None] * frequency
    cosine = jnp.cos(angles)
    sine_part = jnp.sin(angles)
    front_part = vectors[..., :halfway]
    back_part = vectors[..., halfway:]
    return jnp.concatenate(
        [front_part * cosine - back_part * sine_part, back_part * cosine + front_part * sine_part],
        axis=-1,
    )


def online_update(state_in, scores, value_matrix):
    running_max, totals, weighted = state_in
    new_max = jnp.maximum(running_max, jnp.max(scores, axis=-1))
    rescale = jnp.exp(running_max - new_max)
    weight_matrix = jnp.exp(scores - new_max[..., None])
    totals = totals * rescale + jnp.sum(weight_matrix, axis=-1)
    weighted = weighted * rescale[..., None] + jnp.einsum(
        "amz,zav->amv",
        weight_matrix.astype(jnp.bfloat16),
        value_matrix,
        preferred_element_type=jnp.float32,
    )
    return (new_max, totals, weighted)


def attend_windows(query_rows, pool_part, leading_row, req_starts, req_lens, start_state):
    head_width = query_rows.shape[-1]
    kv_local = query_rows.shape[0]
    query_count = query_rows.shape[1]
    req_count = req_starts.shape[0]
    row_span = query_count // req_count
    part_rows = pool_part.shape[0]
    window_rows = min(LONG, part_rows)
    batch_size = math.gcd(req_count, 4)
    batch_count = req_count // batch_size

    def per_request(query_block, begin, length, state_max, state_totals, state_weighted):
        first = jnp.clip(begin - leading_row, 0, part_rows - window_rows)
        window = lax.dynamic_slice_in_dim(pool_part, first, window_rows, 0)
        row_index = leading_row + first + jnp.arange(window_rows, dtype=jnp.int32)
        inside = (row_index >= begin) & (row_index < begin + length)
        scores = jnp.einsum(
            "mjl,wml->mjw",
            query_block,
            window[..., :head_width],
            preferred_element_type=jnp.float32,
        )
        scores = jnp.where(inside[None, None, :], scores, -jnp.inf)
        return online_update(
            (state_max, state_totals, state_weighted), scores, window[..., head_width:]
        )

    def split_requests(array_in):
        moved = jnp.moveaxis(
            array_in.reshape((kv_local, req_count, row_span) + array_in.shape[2:]), 1, 0
        )
        return moved.reshape((batch_count, batch_size) + moved.shape[1:])

    def join_requests(array_in):
        merged = array_in.reshape((req_count,) + array_in.shape[2:])
        return jnp.moveaxis(merged, 0, 1).reshape((kv_local, query_count) + merged.shape[3:])

    def one_batch(inputs):
        return jax.vmap(per_request)(*inputs)

    batched = (
        split_requests(query_rows),
        req_starts.reshape(batch_count, batch_size),
        req_lens.reshape(batch_count, batch_size),
        split_requests(start_state[0]),
        split_requests(start_state[1]),
        split_requests(start_state[2]),
    )
    result = lax.map(one_batch, batched)
    return tuple((join_requests(part_state) for part_state in result))


def local(
    tokens,
    w_query,
    query_bias,
    w_keyval,
    keyval_bias,
    w_out,
    attn_gain,
    final_norm_gain,
    head_weight,
    kv_pool,
    cache_len,
):
    groups = lax.axis_size("req")
    my_group = lax.axis_index("req")
    tp_count = lax.axis_size("tp")
    tp_index = lax.axis_index("tp")
    tok_rows = tokens.shape[0]
    model_width = tokens.shape[1]
    per_group = tok_rows // NEW
    kv_local = kv_pool.shape[1]
    lens_grid = cache_len.reshape(groups, per_group)
    my_lens = lax.dynamic_slice_in_dim(lens_grid, my_group, 1, 0)[0]
    my_starts = jnp.cumsum(my_lens) - my_lens
    source = tokens.astype(jnp.float32)
    mean_square = jnp.mean(source * source, axis=1, keepdims=True)
    normed = (source / jnp.sqrt(mean_square + EPS) * attn_gain[None, :]).astype(jnp.bfloat16)
    query_raw = jnp.dot(normed, w_query, preferred_element_type=jnp.float32) + query_bias[None, :]
    keyval_raw = (
        jnp.dot(normed, w_keyval, preferred_element_type=jnp.float32) + keyval_bias[None, :]
    )
    positions = (my_lens[:, None] + jnp.arange(NEW, dtype=jnp.int32)[None, :]).astype(jnp.float32)
    query_heads = query_raw.reshape(per_group, NEW, kv_local, GROUP, HD)
    queries = (
        rope_rotate(query_heads, positions[:, :, None, None]) * (1.0 / math.sqrt(HD))
    ).astype(jnp.bfloat16)
    keyval_heads = keyval_raw.reshape(per_group, NEW, kv_local, 2, HD)
    key_new = rope_rotate(keyval_heads[:, :, :, 0, :], positions[:, :, None]).astype(jnp.bfloat16)
    value_new = keyval_heads[:, :, :, 1, :].astype(jnp.bfloat16)
    new_kv = jnp.concatenate([key_new, value_new], axis=-1).reshape(tok_rows, kv_local, 2 * HD)
    row_span = NEW * GROUP
    query_count = per_group * row_span
    query_rows = jnp.transpose(queries, (2, 0, 1, 3, 4)).reshape(kv_local, query_count, HD)
    start_state = (
        jnp.full((kv_local, query_count), NEG, jnp.float32),
        jnp.zeros((kv_local, query_count), jnp.float32),
        jnp.zeros((kv_local, query_count, HD), jnp.float32),
    )
    carry_state = attend_windows(query_rows, kv_pool, 0, my_starts, my_lens, start_state)
    key_rows = key_new.reshape(tok_rows, kv_local, HD)
    value_rows = value_new.reshape(tok_rows, kv_local, HD)
    new_scores = jnp.einsum(
        "kqd,mkd->kqm", query_rows, key_rows, preferred_element_type=jnp.float32
    )
    query_token = jnp.arange(query_count, dtype=jnp.int32) // GROUP
    key_token = jnp.arange(tok_rows, dtype=jnp.int32)
    allowed = (query_token[:, None] // NEW == key_token[None, :] // NEW) & (
        key_token[None, :] <= query_token[:, None]
    )
    new_scores = jnp.where(allowed[None], new_scores, -jnp.inf)
    carry_state = online_update(carry_state, new_scores, value_rows)
    attention = (carry_state[2] / carry_state[1][..., None]).astype(jnp.bfloat16)
    attention = jnp.transpose(
        attention.reshape(kv_local, per_group, NEW, GROUP, HD), (1, 2, 0, 3, 4)
    ).reshape(tok_rows, kv_local * GROUP * HD)
    partial_value = jnp.dot(attention, w_out, preferred_element_type=jnp.float32)
    width_local = model_width // tp_count
    summed = lax.psum(partial_value.astype(jnp.bfloat16), "tp").astype(jnp.float32)
    states_full = (source + summed).astype(jnp.bfloat16)
    states = lax.dynamic_slice_in_dim(states_full, tp_index * width_local, width_local, 1)
    last_rows = states_full.reshape(per_group, NEW, model_width)[:, NEW - 1, :].astype(jnp.float32)
    row_norms = jnp.sqrt(jnp.mean(last_rows * last_rows, axis=1) + EPS)
    final_rows = (last_rows / row_norms[:, None] * final_norm_gain[None, :]).astype(jnp.bfloat16)
    logits = jnp.dot(
        lax.all_gather(final_rows, "req", axis=0, tiled=True),
        head_weight,
        preferred_element_type=jnp.float32,
    )
    logit_max = lax.pmax(jnp.max(logits, axis=1), ("req", "tp"))
    return (states, new_kv, row_norms, logit_max, logits)


def solution(mesh):
    return jax.shard_map(
        local,
        mesh=mesh,
        in_specs=(
            P("req", None),
            P(None, "tp"),
            P("tp"),
            P(None, "tp"),
            P("tp"),
            P("tp", None),
            P(),
            P(),
            P(None, ("req", "tp")),
            P("req", "tp", None),
            P(),
        ),
        out_specs=(P("req", "tp"), P("req", "tp", None), P("req"), P(), P(None, ("req", "tp"))),
        check_vma=False,
    )
```

profile of v0, /device:TPU:1, one launch (start us, length us, event | category | flops | bytes accessed | tf_op | source)
XLA Modules:
  0.0 365.2 jit_solution(11805179985593253152)
XLA Ops:
  7.3 3.1 fusion.27
  10.7 3.6 fusion.29
  16.1 4.2 %convolution_add_fusion.1 = f32[384,640]{1,0:T(8,128)} fusion(bf16[384,5120]{1,0:T(8,128)(2,1)S(1)} %fusion.29, bf16[5120,640]{1,0:T(8,128)(2,1)S(1)} %copy-done.12, f32[640]{0:T(1024)S(1)} %copy-done.13), kind=kOutput, calls=%fused_computation.58 | convolution fusion | flops 2516828160 | bytes 11471360 | tf_op jit(solution)/shard_map/dot_general | solution.py:125
  23.5 4.2 %multiply_subtract_fusion = (f32[16,24,1,5,64]{4,3,1,0,2:T(8,128)}, f32[16,24,1,5,64]{4,3,1,0,2:T(8,128)}) fusion(f32[16,24,1,5,128]{4,3,1,0,2:T(8,128)} %reshape.555, f32[16,24,64]{2,1,0:T(8,128)S(1)} %get-tuple-element.120, f32[16,24,64]{2,1,0:T(8,128)S(1)} %get-tuple-element.119), kind=kLoop, calls=%fused_computation.56 | loop fusion | flops 737280 | bytes 2162688 | tf_op jit(solution)/shard_map/sub | solution.py:26
  38.9 3.3 convolution_add_fusion.2
  45.7 81.0 %while.17 = (s32[]{:T(128)}, f32[4,4,1,120]{3,1,2,0:T(4,128)S(1)}, f32[4,4,1,120]{3,1,2,0:T(4,128)S(1)}, f32[4,4,1,120,128]{4,3,1,2,0:T(8,128)}, s32[4,4]{1,0:T(...) while((s32[]{:T(128)}, f32[4,4,1,120]{3,1,2,0:T(4,128)S(1)}, ...), condition=%wide.region_5.6_spmd, body=%wide.region_2.5_spmd.sunk | while | flops 766884224 | bytes 52985684 | solution.py:94
  46.1 12.2 %while.18 = (s32[]{:T(128)}, bf16[26624,1,256]{2,0,1:T(8,128)(2,1)}, s32[4,3]{1,0:T(4,128)S(1)}, bf16[4,3072,1,256]{3,1,2,0:T(8,128)(2,1)}, s32[]{:T(128)}) while((s32[]{:T(128)}, bf16[26624,1,256]{2,0,1:T(8,128)(2,1)}, s32[4,3]{1,0:T(4,128)S(1)}, bf16[4,3072,1,256]{3,1,2,0:T(8,128)(2,1)}, s32[]{:T(128)}) %tuple.62), condition=%wide.while_cond, body=%wide.while_body.sunk | while | flops 2 | bytes 3145833 | solution.py:59
  46.1 3.2 bitcast_dynamic-update-slice_fusion.3
  49.3 3.0 bitcast_dynamic-update-slice_fusion.3
  55.3 3.0 bitcast_dynamic-update-slice_fusion.3
  58.3 4.2 %select_reduce_fusion.2 = (f32[4,120]{1,0:T(4,128)S(1)}, f32[4,120,3072]{2,1,0:T(8,128)S(1)}) fusion(pred[4,3072]{1,0:T(4,128)(4,1)S(1)} %fusion.90, bf16[4,3072,1,256]{3,1,0,2:T(8,128)(2,1)} %bitcast.118, bf16[1,4,1,120,128]{4,1,0,3,2:T(4,128)(2,1)S(1)} %constant_dynamic-slice_fusion.8), kind=kOutput, calls=%fused_computation.3.clone.1 | convolution fusion | flops 380436000 | bytes 9181056 | tf_op jit(solution)/shard_map/while/body/eval_jaxpr/vmap(mjl,wml->mjw)/dot_general | solution.py:62
  66.4 12.1 %while.18 = (s32[]{:T(128)}, bf16[26624,1,256]{2,0,1:T(8,128)(2,1)}, s32[4,3]{1,0:T(4,128)S(1)}, bf16[4,3072,1,256]{3,1,2,0:T(8,128)(2,1)}, s32[]{:T(128)}) while((s32[]{:T(128)}, bf16[26624,1,256]{2,0,1:T(8,128)(2,1)}, s32[4,3]{1,0:T(4,128)S(1)}, bf16[4,3072,1,256]{3,1,2,0:T(8,128)(2,1)}, s32[]{:T(128)}) %tuple.62), condition=%wide.while_cond, body=%wide.while_body.sunk | while | flops 2 | bytes 3145833 | solution.py:59
  66.4 3.0 bitcast_dynamic-update-slice_fusion.3
  75.4 3.0 bitcast_dynamic-update-slice_fusion.3
  78.4 4.2 %select_reduce_fusion.2 = (f32[4,120]{1,0:T(4,128)S(1)}, f32[4,120,3072]{2,1,0:T(8,128)S(1)}) fusion(pred[4,3072]{1,0:T(4,128)(4,1)S(1)} %fusion.90, bf16[4,3072,1,256]{3,1,0,2:T(8,128)(2,1)} %bitcast.118, bf16[1,4,1,120,128]{4,1,0,3,2:T(4,128)(2,1)S(1)} %constant_dynamic-slice_fusion.8), kind=kOutput, calls=%fused_computation.3.clone.1 | convolution fusion | flops 380436000 | bytes 9181056 | tf_op jit(solution)/shard_map/while/body/eval_jaxpr/vmap(mjl,wml->mjw)/dot_general | solution.py:62
  86.5 12.1 %while.18 = (s32[]{:T(128)}, bf16[26624,1,256]{2,0,1:T(8,128)(2,1)}, s32[4,3]{1,0:T(4,128)S(1)}, bf16[4,3072,1,256]{3,1,2,0:T(8,128)(2,1)}, s32[]{:T(128)}) while((s32[]{:T(128)}, bf16[26624,1,256]{2,0,1:T(8,128)(2,1)}, s32[4,3]{1,0:T(4,128)S(1)}, bf16[4,3072,1,256]{3,1,2,0:T(8,128)(2,1)}, s32[]{:T(128)}) %tuple.62), condition=%wide.while_cond, body=%wide.while_body.sunk | while | flops 2 | bytes 3145833 | solution.py:59
  86.5 3.0 bitcast_dynamic-update-slice_fusion.3
  89.6 3.0 bitcast_dynamic-update-slice_fusion.3
  95.6 3.0 bitcast_dynamic-update-slice_fusion.3
  98.6 4.2 %select_reduce_fusion.2 = (f32[4,120]{1,0:T(4,128)S(1)}, f32[4,120,3072]{2,1,0:T(8,128)S(1)}) fusion(pred[4,3072]{1,0:T(4,128)(4,1)S(1)} %fusion.90, bf16[4,3072,1,256]{3,1,0,2:T(8,128)(2,1)} %bitcast.118, bf16[1,4,1,120,128]{4,1,0,3,2:T(4,128)(2,1)S(1)} %constant_dynamic-slice_fusion.8), kind=kOutput, calls=%fused_computation.3.clone.1 | convolution fusion | flops 380436000 | bytes 9181056 | tf_op jit(solution)/shard_map/while/body/eval_jaxpr/vmap(mjl,wml->mjw)/dot_general | solution.py:62
  106.7 12.1 %while.18 = (s32[]{:T(128)}, bf16[26624,1,256]{2,0,1:T(8,128)(2,1)}, s32[4,3]{1,0:T(4,128)S(1)}, bf16[4,3072,1,256]{3,1,2,0:T(8,128)(2,1)}, s32[]{:T(128)}) while((s32[]{:T(128)}, bf16[26624,1,256]{2,0,1:T(8,128)(2,1)}, s32[4,3]{1,0:T(4,128)S(1)}, bf16[4,3072,1,256]{3,1,2,0:T(8,128)(2,1)}, s32[]{:T(128)}) %tuple.62), condition=%wide.while_cond, body=%wide.while_body.sunk | while | flops 2 | bytes 3145833 | solution.py:59
  106.7 3.0 bitcast_dynamic-update-slice_fusion.3
  109.7 3.0 bitcast_dynamic-update-slice_fusion.3
  112.7 3.0 bitcast_dynamic-update-slice_fusion.3
  115.7 3.0 bitcast_dynamic-update-slice_fusion.3
  118.7 4.2 %select_reduce_fusion.2 = (f32[4,120]{1,0:T(4,128)S(1)}, f32[4,120,3072]{2,1,0:T(8,128)S(1)}) fusion(pred[4,3072]{1,0:T(4,128)(4,1)S(1)} %fusion.90, bf16[4,3072,1,256]{3,1,0,2:T(8,128)(2,1)} %bitcast.118, bf16[1,4,1,120,128]{4,1,0,3,2:T(4,128)(2,1)S(1)} %constant_dynamic-slice_fusion.8), kind=kOutput, calls=%fused_computation.3.clone.1 | convolution fusion | flops 380436000 | bytes 9181056 | tf_op jit(solution)/shard_map/while/body/eval_jaxpr/vmap(mjl,wml->mjw)/dot_general | solution.py:62
  129.9 7.6 %convolution_convert_fusion = bf16[384,5120]{1,0:T(8,128)(2,1)} fusion(bf16[384,640]{1,0:T(8,128)(2,1)S(1)} %reshape_transpose_reshape.16, bf16[640,5120]{1,0:T(8,128)(2,1)} %param.18), kind=kOutput, calls=%fused_computation.45 | convolution fusion | flops 2518548480 | bytes 10977280 | tf_op jit(solution)/shard_map/dot_general | solution.py:163
  137.5 91.8 %all-reduce.3.cloned.1.call-done = bf16[384,5120]{1,0:T(8,128)(2,1)} async-done(((bf16[384,5120]{1,0:T(8,128)(2,1)}), bf16[384,5120]{1,0:T(8,128)(2,1)}) %all-reduce.3.cloned.1.call-update) | async-done | bytes 3932176 | tf_op jit(solution)/shard_map/psum | solution.py:165
  229.4 4.8 %fusion.30 = bf16[384,5120]{1,0:T(8,128)(2,1)S(1)} fusion(bf16[384,5120]{1,0:T(8,128)(2,1)} %param.13, bf16[384,5120]{1,0:T(8,128)(2,1)} %all-reduce.3.cloned.1.call-done), kind=kLoop, calls=%fused_computation.44 | loop fusion | flops 7864320 | bytes 11796480 | tf_op jit(solution)/shard_map/convert_element_type | solution.py:166
  240.4 44.9 %all-gather.2.cloned.1.call-done = bf16[512,5120]{1,0:T(8,128)(2,1)} async-done(((bf16[16,5120]{1,0:T(8,128)(2,1)}), bf16[512,5120]{1,0:T(8,128)(2,1)}) %all-gather.2.cloned.1.call-update) | async-done | bytes 5242896 | tf_op jit(solution)/shard_map/all_gather | solution.py:172
  285.3 8.8 %fusion.72 = (f32[512]{0:T(512)S(1)}, f32[512,594]{0,1:T(8,128)}) fusion(bf16[512,5120]{1,0:T(8,128)(2,1)} %all-gather.2.cloned.1.call-done, bf16[5120,594]{0,1:T(8,128)(2,1)} %param.21), kind=kOutput, calls=%fused_computation.122 | convolution fusion | flops 3114574336 | bytes 12544000 | tf_op jit(solution)/shard_map/dot_general | solution.py:171
  294.2 64.1 %pmax.7 = f32[512]{0:T(512)} all-reduce(f32[512]{0:T(512)S(1)} %get-tuple-element.123), channel_id=1, replica_groups=mesh['req'=32,'tp'=4] {'req','tp'}, use_global_device_ids=true, to_apply=%region_11.12 | all-reduce | flops 512 | bytes 4096 | tf_op jit(solution)/shard_map/pmax | solution.py:176
  (150 shorter events, 56.6 us)
Async XLA Ops:
  7.2 31.7 %copy-start = (bf16[5120,256]{1,0:T(8,128)(2,1)S(1)}, bf16[5120,256]{1,0:T(8,128)(2,1)}, u32[]{:S(2)}) copy-start(bf16[5120,256]{1,0:T(8,128)(2,1)} %param.16) | copy-start | bytes 7864324
  7.2 3.3 copy-start.10
  7.2 3.5 copy-start.8
  7.2 222.2 %all-reduce.3.cloned.1.call-start = ((), (), s32[]{:S(2)}) async-start(), calls=%async_computation | async-start | bytes 7864320 | tf_op jit(solution)/shard_map/psum | solution.py:165
  10.6 5.5 %copy-start.12 = (bf16[5120,640]{1,0:T(8,128)(2,1)S(1)}, bf16[5120,640]{1,0:T(8,128)(2,1)}, u32[]{:S(2)}) copy-start(bf16[5120,640]{1,0:T(8,128)(2,1)} %param.14) | copy-start | bytes 19660804
  10.7 5.5 %copy-start.13 = (f32[640]{0:T(1024)S(1)}, f32[640]{0:T(1024)}, u32[]{:S(2)}) copy-start(f32[640]{0:T(1024)} %param.15) | copy-start | bytes 7684
  14.2 1.9 copy-start.4
  30.1 8.8 %copy-start.14 = (f32[256]{0:T(256)S(1)}, f32[256]{0:T(256)}, u32[]{:S(2)}) copy-start(f32[256]{0:T(256)} %param.17) | copy-start | bytes 3076
  45.7 81.2 %copy-start.5 = (f32[1920,64]{1,0:T(8,128)S(1)}, f32[1920,64]{1,0:T(8,128)}, u32[]{:S(2)}) copy-start(f32[1920,64]{1,0:T(8,128)} %concatenate.59) | copy-start | bytes 1474564
  45.7 81.2 %copy-start.6 = (f32[1920,64]{1,0:T(8,128)S(1)}, f32[1920,64]{1,0:T(8,128)}, u32[]{:S(2)}) copy-start(f32[1920,64]{1,0:T(8,128)} %concatenate.60) | copy-start | bytes 1474564
  58.3 4.3 %copy-start.2 = (bf16[4,3072,1,256]{3,1,2,0:T(8,128)(2,1)S(1)}, bf16[4,3072,1,256]{3,1,2,0:T(8,128)(2,1)}, u32[]{:S(2)}) copy-start(bf16[4,3072,1,256]{3,1,2,0:T(8,128)(2,1)} %get-tuple-element.216) | copy-start | bytes 18874372 | tf_op jit(solution)/shard_map/while
  78.4 4.2 %copy-start.2 = (bf16[4,3072,1,256]{3,1,2,0:T(8,128)(2,1)S(1)}, bf16[4,3072,1,256]{3,1,2,0:T(8,128)(2,1)}, u32[]{:S(2)}) copy-start(bf16[4,3072,1,256]{3,1,2,0:T(8,128)(2,1)} %get-tuple-element.216) | copy-start | bytes 18874372 | tf_op jit(solution)/shard_map/while
  98.6 4.2 %copy-start.2 = (bf16[4,3072,1,256]{3,1,2,0:T(8,128)(2,1)S(1)}, bf16[4,3072,1,256]{3,1,2,0:T(8,128)(2,1)}, u32[]{:S(2)}) copy-start(bf16[4,3072,1,256]{3,1,2,0:T(8,128)(2,1)} %get-tuple-element.216) | copy-start | bytes 18874372 | tf_op jit(solution)/shard_map/while
  118.7 4.2 %copy-start.2 = (bf16[4,3072,1,256]{3,1,2,0:T(8,128)(2,1)S(1)}, bf16[4,3072,1,256]{3,1,2,0:T(8,128)(2,1)}, u32[]{:S(2)}) copy-start(bf16[4,3072,1,256]{3,1,2,0:T(8,128)(2,1)} %get-tuple-element.216) | copy-start | bytes 18874372 | tf_op jit(solution)/shard_map/while
  126.9 1.5 copy-start.7
  137.5 99.1 %copy-start.9 = (f32[5120]{0:T(1024)S(1)}, f32[5120]{0:T(1024)}, u32[]{:S(2)}) copy-start(f32[5120]{0:T(1024)} %param.20) | copy-start | bytes 61444
  137.5 147.8 %all-gather.2.cloned.1.call-start = ((), (), s32[]{:S(2)}) async-start(), calls=%async_computation.1 | async-start | bytes 5406720 | tf_op jit(solution)/shard_map/all_gather | solution.py:172
  234.2 1.9 copy-start.3
  236.6 57.6 %copy-start.11 = (f32[16]{0:T(128)}, f32[16]{0:T(128)S(1)}, u32[]{:S(2)}) copy-start(f32[16]{0:T(128)S(1)} %add_sqrt_fusion.1) | copy-start | bytes 196
  285.3 73.0 %copy-start.1 = (bf16[5120,256]{1,0:T(8,128)(2,1)S(1)}, bf16[5120,256]{1,0:T(8,128)(2,1)}, u32[]{:S(2)}) copy-start(bf16[5120,256]{1,0:T(8,128)(2,1)} %param.16) | copy-start | bytes 7864324
Sparse Core Ops, SparseCore 0:
  137.6 91.7 all-reduce.2
  237.5 47.7 all-gather.1
where the time goes:
time: 366 us; the launch traced here: 365 us
  waiting for transfers between devices  137 us (37%)
  local copies, waits for them, and re-layouts  69.7 us (19%)
  blocking collectives  64.1 us (18%)
  matrix products  51.4 us (14%)
  other arithmetic  28.1 us (8%)
  between operations  14.4 us (4%)
    psum x1, waiting for transfers between devices, local(): lax.psum(partial_value.astype(jnp.bfloat16), 'tp').astype(jnp.float32)  91.8 us
    pmax x1, blocking collectives, local(): logit_max = lax.pmax(jnp.max(logits, axis=1), ('req', 'tp'))  64.1 us
    gather x32, local copies, waits for them, and re-layouts  48.3 us
    all_gather x1, waiting for transfers between devices, local(): lax.all_gather(final_rows, 'req', axis=0, tiled=True)  44.9 us
    dot_general x4, matrix products, per_request(): jnp.einsum('mjl,wml->mjw', query_block, window[..., :head_width], preferr...  16.9 us
    dot_general x5, matrix products, online_update(): jnp.einsum('amz,zav->amv', weight_matrix.astype(jnp.bfloat16), value_matr...  9.56 us
    dot_general x1, matrix products, local(): jnp.dot(lax.all_gather(final_rows, 'req', axis=0, tiled=True), head_weigh...  8.84 us
    dot_general x1, matrix products, local(): jnp.dot(attention, w_out, preferred_element_type=jnp.float32)  7.58 us
  transfers between devices with their start and end apart: 2, of which 2 were waited for; matrix products, arithmetic and copies ran while one was open for 1% of the time, Pallas kernels for 0%

commit v1 on v0

--- a/solution.py
+++ b/solution.py
@@ -11,6 +11,12 @@
 THETA = 1000000.0
 EPS = 1e-06
 NEG = -1e30
+
+
+def gather_by_exchange(x, axis, dim):
+    size = lax.axis_size(axis)
+    repeats = [size if d == dim else 1 for d in range(x.ndim)]
+    return lax.all_to_all(jnp.tile(x, repeats), axis, split_axis=dim, concat_axis=dim, tiled=True)
 
 
 def rope_rotate(vectors, positions):
@@ -169,9 +175,7 @@
     row_norms = jnp.sqrt(jnp.mean(last_rows * last_rows, axis=1) + EPS)
     final_rows = (last_rows / row_norms[:, None] * final_norm_gain[None, :]).astype(jnp.bfloat16)
     logits = jnp.dot(
-        lax.all_gather(final_rows, "req", axis=0, tiled=True),
-        head_weight,
-        preferred_element_type=jnp.float32,
+        gather_by_exchange(final_rows, "req", 0), head_weight, preferred_element_type=jnp.float32
     )
     logit_max = lax.pmax(jnp.max(logits, axis=1), ("req", "tp"))
     return (states, new_kv, row_norms, logit_max, logits)

time: 366 us -> 392 us (1.071)
  waiting for transfers between devices: 137 us -> 150 us
  starting transfers between devices: 0.08 us -> 7.76 us
    all_to_all x0 -> x1, waiting for transfers between devices: none -> 58.5 us  [gather_by_exchange(): lax.all_to_all(jnp.tile(x, repeats), axis, split_axis=dim, concat_axis=di...]
    all_gather x1 -> x0, waiting for transfers between devices: 44.9 us -> none  [local(): lax.all_gather(final_rows, 'req', axis=0, tiled=True)]
    all_to_all x0 -> x1, starting transfers between devices: none -> 7.72 us  [gather_by_exchange(): lax.all_to_all(jnp.tile(x, repeats), axis, split_axis=dim, concat_axis=di...]
where the time goes in v1:
time: 392 us; the launch traced here: 391 us
  waiting for transfers between devices  150 us (38%)
  local copies, waits for them, and re-layouts  72.6 us (19%)
  blocking collectives  66.5 us (17%)
  matrix products  51.4 us (13%)
  other arithmetic  27.4 us (7%)
  between operations  14.4 us (4%)
  starting transfers between devices  7.76 us (2%)
    psum x1, waiting for transfers between devices, local(): lax.psum(partial_value.astype(jnp.bfloat16), 'tp').astype(jnp.float32)  91.9 us
    pmax x1, blocking collectives, local(): logit_max = lax.pmax(jnp.max(logits, axis=1), ('req', 'tp'))  66.5 us
    all_to_all x1, waiting for transfers between devices, gather_by_exchange(): lax.all_to_all(jnp.tile(x, repeats), axis, split_axis=dim, concat_axis=di...  58.5 us
    gather x32, local copies, waits for them, and re-layouts  48.2 us
    dot_general x4, matrix products, per_request(): jnp.einsum('mjl,wml->mjw', query_block, window[..., :head_width], preferr...  16.9 us
    dot_general x5, matrix products, online_update(): jnp.einsum('amz,zav->amv', weight_matrix.astype(jnp.bfloat16), value_matr...  9.57 us
    dot_general x1, matrix products, local(): jnp.dot(gather_by_exchange(final_rows, 'req', 0), head_weight, preferred_...  8.84 us
  transfers between devices with their start and end apart: 2, of which 2 were waited for; matrix products, arithmetic and copies ran while one was open for 1% of the time, Pallas kernels for 0%

profile of v1, /device:TPU:1, one launch (start us, length us, event | category | flops | bytes accessed | tf_op | source)
XLA Modules:
  0.0 391.1 jit_solution(7699761293110443719)
XLA Ops:
  7.3 3.1 fusion.27
  10.7 3.6 fusion.29
  16.1 4.2 %convolution_add_fusion.1 = f32[384,640]{1,0:T(8,128)} fusion(bf16[384,5120]{1,0:T(8,128)(2,1)S(1)} %fusion.29, bf16[5120,640]{1,0:T(8,128)(2,1)S(1)} %copy-done.12, f32[640]{0:T(1024)S(1)} %copy-done.13), kind=kOutput, calls=%fused_computation.58 | convolution fusion | flops 2516828160 | bytes 11471360 | tf_op jit(solution)/shard_map/dot_general | solution.py:131
  23.5 4.1 %multiply_subtract_fusion = (f32[16,24,1,5,64]{4,3,1,0,2:T(8,128)}, f32[16,24,1,5,64]{4,3,1,0,2:T(8,128)}) fusion(f32[16,24,1,5,128]{4,3,1,0,2:T(8,128)} %reshape.593, f32[16,24,64]{2,1,0:T(8,128)S(1)} %get-tuple-element.120, f32[16,24,64]{2,1,0:T(8,128)S(1)} %get-tuple-element.119), kind=kLoop, calls=%fused_computation.56 | loop fusion | flops 737280 | bytes 2162688 | tf_op jit(solution)/shard_map/sub | solution.py:32
  38.9 3.3 convolution_add_fusion.2
  45.7 80.9 %while.17 = (s32[]{:T(128)}, f32[4,4,1,120]{3,1,2,0:T(4,128)S(1)}, f32[4,4,1,120]{3,1,2,0:T(4,128)S(1)}, f32[4,4,1,120,128]{4,3,1,2,0:T(8,128)}, s32[4,4]{1,0:T(...) while((s32[]{:T(128)}, f32[4,4,1,120]{3,1,2,0:T(4,128)S(1)}, ...), condition=%wide.region_5.6_spmd, body=%wide.region_2.5_spmd.sunk | while | flops 766884224 | bytes 52985684 | solution.py:100
  46.0 12.2 %while.18 = (s32[]{:T(128)}, bf16[26624,1,256]{2,0,1:T(8,128)(2,1)}, s32[4,3]{1,0:T(4,128)S(1)}, bf16[4,3072,1,256]{3,1,2,0:T(8,128)(2,1)}, s32[]{:T(128)}) while((s32[]{:T(128)}, bf16[26624,1,256]{2,0,1:T(8,128)(2,1)}, s32[4,3]{1,0:T(4,128)S(1)}, bf16[4,3072,1,256]{3,1,2,0:T(8,128)(2,1)}, s32[]{:T(128)}) %tuple.62), condition=%wide.while_cond, body=%wide.while_body.sunk | while | flops 2 | bytes 3145833 | solution.py:65
  46.1 3.2 bitcast_dynamic-update-slice_fusion.3
  49.2 3.0 bitcast_dynamic-update-slice_fusion.3
  55.2 3.0 bitcast_dynamic-update-slice_fusion.3
  58.3 4.2 %select_reduce_fusion.2 = (f32[4,120]{1,0:T(4,128)S(1)}, f32[4,120,3072]{2,1,0:T(8,128)S(1)}) fusion(pred[4,3072]{1,0:T(4,128)(4,1)S(1)} %fusion.90, bf16[4,3072,1,256]{3,1,0,2:T(8,128)(2,1)} %bitcast.119, bf16[1,4,1,120,128]{4,1,0,3,2:T(4,128)(2,1)S(1)} %constant_dynamic-slice_fusion.8), kind=kOutput, calls=%fused_computation.3.clone.1 | convolution fusion | flops 380436000 | bytes 9181056 | tf_op jit(solution)/shard_map/while/body/eval_jaxpr/vmap(mjl,wml->mjw)/dot_general | solution.py:68
  66.3 12.0 %while.18 = (s32[]{:T(128)}, bf16[26624,1,256]{2,0,1:T(8,128)(2,1)}, s32[4,3]{1,0:T(4,128)S(1)}, bf16[4,3072,1,256]{3,1,2,0:T(8,128)(2,1)}, s32[]{:T(128)}) while((s32[]{:T(128)}, bf16[26624,1,256]{2,0,1:T(8,128)(2,1)}, s32[4,3]{1,0:T(4,128)S(1)}, bf16[4,3072,1,256]{3,1,2,0:T(8,128)(2,1)}, s32[]{:T(128)}) %tuple.62), condition=%wide.while_cond, body=%wide.while_body.sunk | while | flops 2 | bytes 3145833 | solution.py:65
  66.4 3.0 bitcast_dynamic-update-slice_fusion.3
  69.4 3.0 bitcast_dynamic-update-slice_fusion.3
  75.4 3.0 bitcast_dynamic-update-slice_fusion.3
  78.4 4.2 %select_reduce_fusion.2 = (f32[4,120]{1,0:T(4,128)S(1)}, f32[4,120,3072]{2,1,0:T(8,128)S(1)}) fusion(pred[4,3072]{1,0:T(4,128)(4,1)S(1)} %fusion.90, bf16[4,3072,1,256]{3,1,0,2:T(8,128)(2,1)} %bitcast.119, bf16[1,4,1,120,128]{4,1,0,3,2:T(4,128)(2,1)S(1)} %constant_dynamic-slice_fusion.8), kind=kOutput, calls=%fused_computation.3.clone.1 | convolution fusion | flops 380436000 | bytes 9181056 | tf_op jit(solution)/shard_map/while/body/eval_jaxpr/vmap(mjl,wml->mjw)/dot_general | solution.py:68
  86.5 12.0 %while.18 = (s32[]{:T(128)}, bf16[26624,1,256]{2,0,1:T(8,128)(2,1)}, s32[4,3]{1,0:T(4,128)S(1)}, bf16[4,3072,1,256]{3,1,2,0:T(8,128)(2,1)}, s32[]{:T(128)}) while((s32[]{:T(128)}, bf16[26624,1,256]{2,0,1:T(8,128)(2,1)}, s32[4,3]{1,0:T(4,128)S(1)}, bf16[4,3072,1,256]{3,1,2,0:T(8,128)(2,1)}, s32[]{:T(128)}) %tuple.62), condition=%wide.while_cond, body=%wide.while_body.sunk | while | flops 2 | bytes 3145833 | solution.py:65
  86.5 3.0 bitcast_dynamic-update-slice_fusion.3
  89.5 3.0 bitcast_dynamic-update-slice_fusion.3
  95.5 3.0 bitcast_dynamic-update-slice_fusion.3
  98.5 4.2 %select_reduce_fusion.2 = (f32[4,120]{1,0:T(4,128)S(1)}, f32[4,120,3072]{2,1,0:T(8,128)S(1)}) fusion(pred[4,3072]{1,0:T(4,128)(4,1)S(1)} %fusion.90, bf16[4,3072,1,256]{3,1,0,2:T(8,128)(2,1)} %bitcast.119, bf16[1,4,1,120,128]{4,1,0,3,2:T(4,128)(2,1)S(1)} %constant_dynamic-slice_fusion.8), kind=kOutput, calls=%fused_computation.3.clone.1 | convolution fusion | flops 380436000 | bytes 9181056 | tf_op jit(solution)/shard_map/while/body/eval_jaxpr/vmap(mjl,wml->mjw)/dot_general | solution.py:68
  106.6 12.0 %while.18 = (s32[]{:T(128)}, bf16[26624,1,256]{2,0,1:T(8,128)(2,1)}, s32[4,3]{1,0:T(4,128)S(1)}, bf16[4,3072,1,256]{3,1,2,0:T(8,128)(2,1)}, s32[]{:T(128)}) while((s32[]{:T(128)}, bf16[26624,1,256]{2,0,1:T(8,128)(2,1)}, s32[4,3]{1,0:T(4,128)S(1)}, bf16[4,3072,1,256]{3,1,2,0:T(8,128)(2,1)}, s32[]{:T(128)}) %tuple.62), condition=%wide.while_cond, body=%wide.while_body.sunk | while | flops 2 | bytes 3145833 | solution.py:65
  106.6 3.0 bitcast_dynamic-update-slice_fusion.3
  115.6 3.0 bitcast_dynamic-update-slice_fusion.3
  118.6 4.2 %select_reduce_fusion.2 = (f32[4,120]{1,0:T(4,128)S(1)}, f32[4,120,3072]{2,1,0:T(8,128)S(1)}) fusion(pred[4,3072]{1,0:T(4,128)(4,1)S(1)} %fusion.90, bf16[4,3072,1,256]{3,1,0,2:T(8,128)(2,1)} %bitcast.119, bf16[1,4,1,120,128]{4,1,0,3,2:T(4,128)(2,1)S(1)} %constant_dynamic-slice_fusion.8), kind=kOutput, calls=%fused_computation.3.clone.1 | convolution fusion | flops 380436000 | bytes 9181056 | tf_op jit(solution)/shard_map/while/body/eval_jaxpr/vmap(mjl,wml->mjw)/dot_general | solution.py:68
  129.8 7.6 %convolution_convert_fusion = bf16[384,5120]{1,0:T(8,128)(2,1)} fusion(bf16[384,640]{1,0:T(8,128)(2,1)S(1)} %reshape_transpose_reshape.16, bf16[640,5120]{1,0:T(8,128)(2,1)} %param.18), kind=kOutput, calls=%fused_computation.45 | convolution fusion | flops 2518548480 | bytes 10977280 | tf_op jit(solution)/shard_map/dot_general | solution.py:169
  137.4 91.9 %all-reduce.3.cloned.1.call-done = bf16[384,5120]{1,0:T(8,128)(2,1)} async-done(((bf16[384,5120]{1,0:T(8,128)(2,1)}), bf16[384,5120]{1,0:T(8,128)(2,1)}) %all-reduce.3.cloned.1.call-update) | async-done | bytes 3932176 | tf_op jit(solution)/shard_map/psum | solution.py:171
  229.3 4.8 %fusion.30 = bf16[384,5120]{1,0:T(8,128)(2,1)S(1)} fusion(bf16[384,5120]{1,0:T(8,128)(2,1)} %param.13, bf16[384,5120]{1,0:T(8,128)(2,1)} %all-reduce.3.cloned.1.call-done), kind=kLoop, calls=%fused_computation.44 | loop fusion | flops 7864320 | bytes 11796480 | tf_op jit(solution)/shard_map/convert_element_type | solution.py:172
  239.6 7.7 %all-to-all-start = ((bf16[32,16,5120]{2,1,0:T(8,128)(2,1)}), bf16[32,16,5120]{2,1,0:T(8,128)(2,1)}, u32[]{:S(2)}, u32[]{:S(2)}) async-start(bf16[32,16,5120]{2,1,0:T(8,128)(2,1)} %tile.2), calls=%async_computation | async-start | bytes 10485760 | tf_op jit(solution)/shard_map/all_to_all | solution.py:19
  250.4 58.5 %all-to-all-done = bf16[32,16,5120]{2,1,0:T(8,128)(2,1)} async-done(((bf16[32,16,5120]{2,1,0:T(8,128)(2,1)}), bf16[32,16,5120]{2,1,0:T(8,128)(2,1)}, u32[]{:S(2)}, u32[]{:S(2)}) %all-to-all-start) | async-done | bytes 5242912 | tf_op jit(solution)/shard_map/all_to_all | solution.py:19
  308.9 8.8 %fusion.72 = (f32[512]{0:T(512)S(1)}, f32[512,594]{0,1:T(8,128)}) fusion(bf16[512,5120]{1,0:T(8,128)(2,1)} %bitcast.24, bf16[5120,594]{0,1:T(8,128)(2,1)} %param.21), kind=kOutput, calls=%fused_computation.122 | convolution fusion | flops 3114574336 | bytes 12544000 | tf_op jit(solution)/shard_map/dot_general | solution.py:177
  317.7 66.5 %pmax.7 = f32[512]{0:T(512)} all-reduce(f32[512]{0:T(512)S(1)} %get-tuple-element.123), channel_id=1, replica_groups=mesh['req'=32,'tp'=4] {'req','tp'}, use_global_device_ids=true, to_apply=%region_11.12 | all-reduce | flops 512 | bytes 4096 | tf_op jit(solution)/shard_map/pmax | solution.py:180
  (150 shorter events, 61.9 us)
Async XLA Ops:
  7.2 31.7 %copy-start = (bf16[5120,256]{1,0:T(8,128)(2,1)S(1)}, bf16[5120,256]{1,0:T(8,128)(2,1)}, u32[]{:S(2)}) copy-start(bf16[5120,256]{1,0:T(8,128)(2,1)} %param.16) | copy-start | bytes 7864324
  7.2 3.3 copy-start.10
  7.2 3.5 copy-start.8
  7.2 222.1 %all-reduce.3.cloned.1.call-start = ((), (), s32[]{:S(2)}) async-start(), calls=%async_computation.1 | async-start | bytes 7864320 | tf_op jit(solution)/shard_map/psum | solution.py:171
  10.6 5.5 %copy-start.12 = (bf16[5120,640]{1,0:T(8,128)(2,1)S(1)}, bf16[5120,640]{1,0:T(8,128)(2,1)}, u32[]{:S(2)}) copy-start(bf16[5120,640]{1,0:T(8,128)(2,1)} %param.14) | copy-start | bytes 19660804
  10.7 5.5 %copy-start.13 = (f32[640]{0:T(1024)S(1)}, f32[640]{0:T(1024)}, u32[]{:S(2)}) copy-start(f32[640]{0:T(1024)} %param.15) | copy-start | bytes 7684
  14.2 1.9 copy-start.4
  30.0 8.8 %copy-start.14 = (f32[256]{0:T(256)S(1)}, f32[256]{0:T(256)}, u32[]{:S(2)}) copy-start(f32[256]{0:T(256)} %param.17) | copy-start | bytes 3076
  45.7 81.1 %copy-start.5 = (f32[1920,64]{1,0:T(8,128)S(1)}, f32[1920,64]{1,0:T(8,128)}, u32[]{:S(2)}) copy-start(f32[1920,64]{1,0:T(8,128)} %concatenate.59) | copy-start | bytes 1474564
  45.7 81.1 %copy-start.6 = (f32[1920,64]{1,0:T(8,128)S(1)}, f32[1920,64]{1,0:T(8,128)}, u32[]{:S(2)}) copy-start(f32[1920,64]{1,0:T(8,128)} %concatenate.60) | copy-start | bytes 1474564
  58.3 4.2 %copy-start.2 = (bf16[4,3072,1,256]{3,1,2,0:T(8,128)(2,1)S(1)}, bf16[4,3072,1,256]{3,1,2,0:T(8,128)(2,1)}, u32[]{:S(2)}) copy-start(bf16[4,3072,1,256]{3,1,2,0:T(8,128)(2,1)} %get-tuple-element.216) | copy-start | bytes 18874372 | tf_op jit(solution)/shard_map/while
  78.4 4.3 %copy-start.2 = (bf16[4,3072,1,256]{3,1,2,0:T(8,128)(2,1)S(1)}, bf16[4,3072,1,256]{3,1,2,0:T(8,128)(2,1)}, u32[]{:S(2)}) copy-start(bf16[4,3072,1,256]{3,1,2,0:T(8,128)(2,1)} %get-tuple-element.216) | copy-start | bytes 18874372 | tf_op jit(solution)/shard_map/while
  98.5 4.3 %copy-start.2 = (bf16[4,3072,1,256]{3,1,2,0:T(8,128)(2,1)S(1)}, bf16[4,3072,1,256]{3,1,2,0:T(8,128)(2,1)}, u32[]{:S(2)}) copy-start(bf16[4,3072,1,256]{3,1,2,0:T(8,128)(2,1)} %get-tuple-element.216) | copy-start | bytes 18874372 | tf_op jit(solution)/shard_map/while
  118.6 4.3 %copy-start.2 = (bf16[4,3072,1,256]{3,1,2,0:T(8,128)(2,1)S(1)}, bf16[4,3072,1,256]{3,1,2,0:T(8,128)(2,1)}, u32[]{:S(2)}) copy-start(bf16[4,3072,1,256]{3,1,2,0:T(8,128)(2,1)} %get-tuple-element.216) | copy-start | bytes 18874372 | tf_op jit(solution)/shard_map/while
  126.8 1.5 copy-start.7
  137.4 99.1 %copy-start.9 = (f32[5120]{0:T(1024)S(1)}, f32[5120]{0:T(1024)}, u32[]{:S(2)}) copy-start(f32[5120]{0:T(1024)} %param.20) | copy-start | bytes 61444
  234.1 2.0 copy-start.3
  236.5 3.1 copy-start.11
  239.6 69.2 %all-to-all-start = ((bf16[32,16,5120]{2,1,0:T(8,128)(2,1)}), bf16[32,16,5120]{2,1,0:T(8,128)(2,1)}, u32[]{:S(2)}, u32[]{:S(2)}) async-start(bf16[32,16,5120]{2,1,0:T(8,128)(2,1)} %tile.2), calls=%async_computation | async-start | bytes 10485760 | tf_op jit(solution)/shard_map/all_to_all | solution.py:19
  308.9 75.4 %copy-start.1 = (bf16[5120,256]{1,0:T(8,128)(2,1)S(1)}, bf16[5120,256]{1,0:T(8,128)(2,1)}, u32[]{:S(2)}) copy-start(bf16[5120,256]{1,0:T(8,128)(2,1)} %param.16) | copy-start | bytes 7864324
Sparse Core Ops, SparseCore 0:
  137.5 91.7 all-reduce.2
